TPU v7x, 256 devices: a whole 4x4x8 slice. The times are simulated.
256 devices in a mesh: fsdp: 8 (over x, y_hi), frame: 32 (over y_lo, z, core).
Axes of the slice: x: 4, y: 4 (y_hi: 2, y_lo: 2; y = y_hi * 2 + y_lo), z: 8, core: 2. Of those that a mesh axis runs over, the one named last changes fastest.
Arguments:
- queries: bfloat16 [32, 1024, 1024], P('frame', 'fsdp'), may hold values from -5 to 5
- key_rows: bfloat16 [32, 1024, 1024], P('frame', 'fsdp'), may hold values from -5 to 5
- value_rows: bfloat16 [32, 1024, 1024], P('frame', 'fsdp'), may hold values from -6 to 6
- out_weight: bfloat16 [1024, 2048], P(('fsdp', 'frame')), may hold values from -0.75 to 0.75
- conv_weight: bfloat16 [31, 2048], replicated, may hold values from -1 to 1
- grad_out: bfloat16 [32, 1024, 2048], P('frame', 'fsdp'), may hold values from -6 to 6
Outputs:
- block_out: bfloat16 [32, 1024, 2048], P('frame', 'fsdp')
- grad_queries: bfloat16 [32, 1024, 1024], P('frame', 'fsdp')
- grad_keys: bfloat16 [32, 1024, 1024], P('frame', 'fsdp')
- grad_values: bfloat16 [32, 1024, 1024], P('frame', 'fsdp')
- weight_grad: float32 [1024, 2048], P(('fsdp', 'frame'))
- conv_grad: float32 [31, 2048], replicated
All inputs are finite; a program needn't handle non-finite values.
Results may differ from a plain program's by a relative error of at most 0.014.
Values may be sent and summed in bfloat16 or wider, within the bound.
A program may use at most 128 MiB of HBM per device.

v0:
```python
import math
import jax
import jax.numpy as jnp
from jax import lax
from jax.sharding import PartitionSpec as P

HEADS = 8
HDIM = 128
KERNEL = 31


def with_halo(cells, sides, width):
    for axis, dim in sides:
        count = lax.axis_size(axis)
        ends = count - 1
        head = lax.slice_in_dim(cells, 0, width, axis=dim)
        tail = lax.slice_in_dim(cells, cells.shape[dim] - width, cells.shape[dim], axis=dim)
        cells = jnp.concatenate(
            [
                lax.ppermute(tail, axis, [(i, (i + 1) % count) for i in range(ends)]),
                cells,
                lax.ppermute(head, axis, [((i + 1) % count, i) for i in range(ends)]),
            ],
            axis=dim,
        )
    return cells


def head_scores(queries, key_rows):
    return jnp.einsum("qd,kd->qk", queries, key_rows, preferred_element_type=jnp.float32) * (
        1.0 / math.sqrt(HDIM)
    )


def forward_head(queries, key_rows, value_rows):
    scores = head_scores(queries, key_rows)
    row_max = jnp.max(scores, axis=1)
    exponent = jnp.exp(scores - row_max[:, None])
    row_sum = jnp.sum(exponent, axis=1)
    rounded = (exponent / row_sum[:, None]).astype(jnp.bfloat16)
    attended = jnp.dot(rounded, value_rows, preferred_element_type=jnp.float32).astype(jnp.bfloat16)
    return (attended, row_max, row_sum)


def score_grads(queries, key_rows, value_rows, upstream, row_max, row_sum, row_dot):
    scores = head_scores(queries, key_rows)
    weights = jnp.exp(scores - row_max[:, None]) / row_sum[:, None]
    grad_probs = jnp.einsum("qd,kd->qk", upstream, value_rows, preferred_element_type=jnp.float32)
    if row_dot is None:
        row_dot = jnp.sum(weights * grad_probs, axis=1)
    grad_scores = (weights * (grad_probs - row_dot[:, None])).astype(jnp.bfloat16)
    return (weights, grad_scores, row_dot)


def query_grad(grad_scores, key_rows):
    product = jnp.dot(grad_scores, key_rows, preferred_element_type=jnp.float32)
    return (product * (1.0 / math.sqrt(HDIM))).astype(jnp.bfloat16)


def key_grads(queries, weights, grad_scores, upstream):
    grad_key = jnp.einsum("qk,qd->kd", grad_scores, queries, preferred_element_type=jnp.float32) * (
        1.0 / math.sqrt(HDIM)
    )
    grad_value = jnp.einsum(
        "qk,qd->kd", weights.astype(jnp.bfloat16), upstream, preferred_element_type=jnp.float32
    )
    return (grad_key, grad_value)


def depthwise(signal, taps):
    channels = signal.shape[1]
    result = lax.conv_general_dilated(
        signal[None],
        taps[:, None, :],
        (1,),
        "VALID",
        dimension_numbers=("NWC", "WIO", "NWC"),
        feature_group_count=channels,
        precision=lax.Precision.HIGHEST,
        preferred_element_type=jnp.float32,
    )
    return result[0]


def shards(queries, key_rows, value_rows, out_weight, conv_weight, grad_out):
    local_rows = queries.shape[1]
    half_width = KERNEL // 2
    own_queries = queries[0]
    own_keys = key_rows[0]
    own_values = value_rows[0]
    upstream = grad_out[0].astype(jnp.float32)
    full_weight = lax.all_gather(out_weight, ("fsdp", "frame"), axis=0, tiled=True)
    groups = lax.axis_size("fsdp")
    all_keys, all_values = (
        lax.all_gather(own_keys, "fsdp", axis=0, tiled=True),
        lax.all_gather(own_values, "fsdp", axis=0, tiled=True),
    )
    pieces = []
    maxima = []
    row_sums = []
    for head_index in range(HEADS):
        columns = slice(head_index * HDIM, (head_index + 1) * HDIM)
        attended, row_max, row_sum = forward_head(
            own_queries[:, columns], all_keys[:, columns], all_values[:, columns]
        )
        pieces.append(attended)
        maxima.append(row_max)
        row_sums.append(row_sum)
    attention = jnp.concatenate(pieces, axis=1)
    row_maxes = jnp.stack(maxima, axis=1)
    row_totals = jnp.stack(row_sums, axis=1)
    projected = jnp.dot(attention, full_weight, preferred_element_type=jnp.float32).astype(
        jnp.bfloat16
    )
    padded = with_halo(projected[None], (("fsdp", 1),), half_width)[0].astype(jnp.float32)
    conv_taps = conv_weight.astype(jnp.float32)
    conv_value = depthwise(padded, conv_taps)
    sigmoid_conv = jax.nn.sigmoid(conv_value)
    block_out = (padded[half_width : half_width + local_rows] + conv_value * sigmoid_conv).astype(
        jnp.bfloat16
    )
    grad_conv = (upstream * sigmoid_conv * (1.0 + conv_value * (1.0 - sigmoid_conv))).astype(
        jnp.bfloat16
    )
    grad_padded = with_halo(grad_conv[None], (("fsdp", 1),), half_width)[0].astype(jnp.float32)
    grad_projected = (upstream + depthwise(grad_padded, conv_taps[::-1])).astype(jnp.bfloat16)
    conv_terms = depthwise(padded, grad_conv.astype(jnp.float32))
    total_frames = local_rows * groups * lax.axis_size("frame")
    grad_scale = 1.0 / math.sqrt(total_frames)
    conv_grad = lax.psum(conv_terms, ("fsdp", "frame")) * grad_scale
    weight_grad = (
        lax.psum_scatter(
            jnp.einsum("ri,rd->id", attention, grad_projected, preferred_element_type=jnp.float32),
            ("fsdp", "frame"),
            scatter_dimension=0,
            tiled=True,
        )
        * grad_scale
    )
    grad_attention = jnp.einsum(
        "rd,id->ri", grad_projected, full_weight, preferred_element_type=jnp.float32
    ).astype(jnp.bfloat16)
    query_list = []
    row_dots = []
    for head_index in range(HEADS):
        columns = slice(head_index * HDIM, (head_index + 1) * HDIM)
        weights, grad_scores, row_dot = score_grads(
            own_queries[:, columns],
            all_keys[:, columns],
            all_values[:, columns],
            grad_attention[:, columns],
            row_maxes[:, head_index],
            row_totals[:, head_index],
            None,
        )
        query_list.append(query_grad(grad_scores, all_keys[:, columns]))
        row_dots.append(row_dot)
    row_dot_table = jnp.stack(row_dots, axis=1)
    span_queries, span_grads = (
        lax.all_gather(own_queries, "fsdp", axis=0, tiled=True),
        lax.all_gather(grad_attention, "fsdp", axis=0, tiled=True),
    )
    span_max, span_sum, span_dot = (
        lax.all_gather(row_maxes, "fsdp", axis=0, tiled=True),
        lax.all_gather(row_totals, "fsdp", axis=0, tiled=True),
        lax.all_gather(row_dot_table, "fsdp", axis=0, tiled=True),
    )
    key_list = []
    value_list = []
    for head_index in range(HEADS):
        columns = slice(head_index * HDIM, (head_index + 1) * HDIM)
        weights, grad_scores, unused_dot = score_grads(
            span_queries[:, columns],
            own_keys[:, columns],
            own_values[:, columns],
            span_grads[:, columns],
            span_max[:, head_index],
            span_sum[:, head_index],
            span_dot[:, head_index],
        )
        grad_key, grad_value = key_grads(
            span_queries[:, columns], weights, grad_scores, span_grads[:, columns]
        )
        key_list.append(grad_key.astype(jnp.bfloat16))
        value_list.append(grad_value.astype(jnp.bfloat16))
    grad_queries = jnp.concatenate(query_list, axis=1)
    grad_keys = jnp.concatenate(key_list, axis=1)
    grad_values = jnp.concatenate(value_list, axis=1)
    return (
        block_out[None],
        grad_queries[None],
        grad_keys[None],
        grad_values[None],
        weight_grad,
        conv_grad,
    )


def solution(mesh):
    return jax.shard_map(
        shards,
        mesh=mesh,
        in_specs=(
            P("frame", "fsdp", None),
            P("frame", "fsdp", None),
            P("frame", "fsdp", None),
            P(("fsdp", "frame"), None),
            P(),
            P("frame", "fsdp", None),
        ),
        out_specs=(
            P("frame", "fsdp", None),
            P("frame", "fsdp", None),
            P("frame", "fsdp", None),
            P("frame", "fsdp", None),
            P(("fsdp", "frame"), None),
            P(),
        ),
        check_vma=False,
    )
```

profile of v0, /device:TPU:97, one launch (start us, length us, event | category | flops | bytes accessed | tf_op | source)
XLA Modules:
  0.0 727.7 jit_solution(12551051840050109042)
XLA Ops:
  10.0 7.9 %rev.3 = f32[31,2048]{1,0:T(8,128)} reverse(bf16[31,2048]{1,0:T(8,128)(2,1)} %param.10), dimensions={0} | reverse | bytes 380928 | tf_op jit(solution)/shard_map/rev | solution.py:126
  17.9 53.3 %all-gather.12.cloned.1.call-done = bf16[1,1024,1024]{2,1,0:T(8,128)(2,1)} async-done(((bf16[1,128,1024]{2,1,0:T(8,128)(2,1)}), bf16[1,1024,1024]{2,1,0:T(8,128)(2,1)}) %all-gather.12.cloned.1.call-update) | async-done | bytes 2097168 | tf_op jit(solution)/shard_map/all_gather | solution.py:95
  84.2 27.9 %all_gather.29 = f32[1024,8]{0,1:T(8,128)S(1)} all-gather(f32[128,8]{0,1:T(8,128)S(1)} %stack.7), channel_id=1, replica_groups=mesh['fsdp'=8,'frame'=32] {'fsdp'}, dimensions={0}, use_global_device_ids=true | all-gather | bytes 36864 | tf_op jit(solution)/shard_map/all_gather | solution.py:165
  112.1 28.1 %all_gather.28 = f32[1024,8]{0,1:T(8,128)S(1)} all-gather(f32[128,8]{0,1:T(8,128)S(1)} %stack.6), channel_id=1, replica_groups=mesh['fsdp'=8,'frame'=32] {'fsdp'}, dimensions={0}, use_global_device_ids=true | all-gather | bytes 36864 | tf_op jit(solution)/shard_map/all_gather | solution.py:164
  145.4 49.5 %all-gather.16.cloned.1.call-done = bf16[1,1024,1024]{2,1,0:T(8,128)(2,1)} async-done(((bf16[1,128,1024]{2,1,0:T(8,128)(2,1)}), bf16[1,1024,1024]{2,1,0:T(8,128)(2,1)}) %all-gather.16.cloned.1.call-update) | async-done | bytes 2097168 | tf_op jit(solution)/shard_map/all_gather | solution.py:160
  194.9 2.3 fusion.8
  204.3 109.2 %all-gather.18.cloned.1.call-done = bf16[256,4,2048]{2,1,0:T(4,128)(2,1)} async-done(((bf16[1,4,2048]{2,1,0:T(4,128)(2,1)}), bf16[256,4,2048]{2,1,0:T(4,128)(2,1)}) %all-gather.18.cloned.1.call-update) | async-done | bytes 4194320 | tf_op jit(solution)/shard_map/all_gather | solution.py:92
  313.6 6.9 reshape.105
  320.5 2.9 convolution_convert_fusion
  324.9 5.5 collective-permute-start
  330.4 2.1 fusion.36
  332.7 8.1 %multiply_convert_fusion = (bf16[1,128,2048]{2,0,1:T(2,128)(2,1)S(1)}, f32[1,128,2048]{2,0,1:T(1,128)S(1)}) fusion(bf16[1,128,2048]{2,1,0:T(8,128)(2,1)S(1)} %copy-done.26, bf16[31,1,2048]{2,0,1:T(8,128)(2,1)S(1)} %bitcast.163, bf16[1,158,2048]{2,1,0:T(8,128)(2,1)S(1)} %pad_maximum_fusion), kind=kOutput, calls=%fused_computation.178 | convolution fusion | flops 18874368 | bytes 2871296 | tf_op jit(solution)/shard_map/conv_general_dilated | solution.py:72
  342.4 6.3 collective-permute-start.2
  348.7 7.4 %fusion.119 = f32[1,31,2048]{2,0,1:T(1,128)S(1)} fusion(f32[1,128,2048]{2,0,1:T(1,128)S(1)} %get-tuple-element.65, bf16[1,158,2048]{2,1,0:T(8,128)(2,1)S(1)} %pad_maximum_fusion, bf16[1,128,2048]{2,1,0:T(8,128)(2,1)S(1)} %copy-done.26), kind=kOutput, calls=%fused_computation.176 | convolution fusion | flops 18874368 | bytes 2473984 | tf_op jit(solution)/shard_map/conv_general_dilated | solution.py:72
  358.3 4.9 fusion
  364.2 2.3 convolution_convert_fusion.1
  366.5 2.2 multiply_reduce_fusion.7
  368.8 2.0 multiply_reduce_fusion.6
  382.7 4.5 fusion.126
  388.2 2.0 fusion.93
  392.1 30.5 %all_gather.31 = f32[1024,8]{0,1:T(8,128)S(1)} all-gather(f32[128,8]{0,1:T(8,128)S(1)} %stack.8), channel_id=1, replica_groups=mesh['fsdp'=8,'frame'=32] {'fsdp'}, dimensions={0}, use_global_device_ids=true | all-gather | bytes 36864 | tf_op jit(solution)/shard_map/all_gather | solution.py:166
  422.6 9.0 %all-gather.10.cloned.1.call-done = bf16[1024,1024]{1,0:T(8,128)(2,1)} async-done(((bf16[128,1024]{1,0:T(8,128)(2,1)}), bf16[1024,1024]{1,0:T(8,128)(2,1)}) %all-gather.10.cloned.1.call-update) | async-done | bytes 2097168 | tf_op jit(solution)/shard_map/all_gather | solution.py:161
  431.7 2.3 fusion.63
  433.9 2.1 fusion.65
  436.0 2.2 fusion.67
  438.2 2.2 fusion.69
  440.4 2.2 fusion.71
  442.6 2.2 fusion.73
  444.8 2.2 fusion.75
  446.9 2.2 fusion.77
  449.1 1.8 copy.26
  455.4 262.4 %all-reduce.4.cloned.1.call-done = (f32[1024,2048]{1,0:T(8,128)}, f32[31,2048]{1,0:T(8,128)}) async-done(((f32[1024,2048]{1,0:T(8,128)}, f32[31,2048]{1,0:T(8,128)}), (f32[1024,2048]{1,0:T(8,128)}, f32[31,2048]{1,0:T(8,128)})) %all-reduce.4.cloned.1.call-update) | async-done | bytes 8642576
  (145 shorter events, 56.6 us)
Async XLA Ops:
  7.2 64.0 %all-gather.12.cloned.1.call-start = ((), (), s32[]{:S(2)}) async-start(), calls=%async_computation.1 | async-start | bytes 2359296 | tf_op jit(solution)/shard_map/all_gather | solution.py:95
  7.9 132.4 %all-gather.14.cloned.1.call-start = ((), (), s32[]{:S(2)}) async-start(), calls=%async_computation.2 | async-start | bytes 2359296 | tf_op jit(solution)/shard_map/all_gather | solution.py:96
  8.6 186.2 %all-gather.16.cloned.1.call-start = ((), (), s32[]{:S(2)}) async-start(), calls=%async_computation.3 | async-start | bytes 2359296 | tf_op jit(solution)/shard_map/all_gather | solution.py:160
  9.4 304.2 %all-gather.18.cloned.1.call-start = ((), (), s32[]{:S(2)}) async-start(), calls=%async_computation.4 | async-start | bytes 4210688 | tf_op jit(solution)/shard_map/all_gather | solution.py:92
  10.0 421.7 %all-gather.10.cloned.1.call-start = ((), (), s32[]{:S(2)}) async-start(), calls=%async_computation | async-start | bytes 2359296 | tf_op jit(solution)/shard_map/all_gather | solution.py:161
  74.8 4.8 copy-start.2
  140.3 2.9 copy-start.24
  194.9 2.3 copy-start.20
  194.9 2.3 copy-start.23
  323.4 9.3 %copy-start.22 = (bf16[31,2048]{1,0:T(8,128)(2,1)S(1)}, bf16[31,2048]{1,0:T(8,128)(2,1)}, u32[]{:S(2)}) copy-start(bf16[31,2048]{1,0:T(8,128)(2,1)} %param.10) | copy-start | bytes 380932
  323.4 9.3 %copy-start.26 = (bf16[1,128,2048]{2,1,0:T(8,128)(2,1)S(1)}, bf16[1,128,2048]{2,1,0:T(8,128)(2,1)}, u32[]{:S(2)}) copy-start(bf16[1,128,2048]{2,1,0:T(8,128)(2,1)} %param.11) | copy-start | bytes 1572868
  323.4 9.1 %collective-permute-start.1 = (bf16[1,15,2048]{2,1,0:T(8,128)(2,1)S(1)}, bf16[1,15,2048]{2,1,0:T(8,128)(2,1)S(1)}, u32[]{:S(2)}, u32[]{:S(2)}) collective-permute-start(bf16[1,15,2048]{2,1,0:T(8,128)(2,1)S(1)} %get-tuple-element.23), channel_id=1, source_target_pairs={{32,0},{64,32},{96,64},{128,96},{160,128},{192,160},{224,192},{33,... | collective-permute-start | bytes 184328 | tf_op jit(solution)/shard_map/ppermute | solution.py:22
  324.9 7.6 %collective-permute-start = (bf16[1,15,2048]{2,1,0:T(8,128)(2,1)S(1)}, bf16[1,15,2048]{2,1,0:T(8,128)(2,1)S(1)}, u32[]{:S(2)}, u32[]{:S(2)}) collective-permute-start(bf16[1,15,2048]{2,1,0:T(8,128)(2,1)S(1)} %get-tuple-element.22), channel_id=1, source_target_pairs={{0,32},{32,64},{64,96},{96,128},{128,160},{160,192},{192,224},{1,3... | collective-permute-start | bytes 184328 | tf_op jit(solution)/shard_map/ppermute | solution.py:20
  341.1 17.2 %collective-permute-start.3 = (bf16[1,15,2048]{2,0,1:T(2,128)(2,1)S(1)}, bf16[1,15,2048]{2,0,1:T(2,128)(2,1)S(1)}, u32[]{:S(2)}, u32[]{:S(2)}) collective-permute-start(bf16[1,15,2048]{2,0,1:T(2,128)(2,1)S(1)} %get-tuple-element.21), channel_id=1, source_target_pairs={{32,0},{64,32},{96,64},{128,96},{160,128},{192,160},{224,192},{33,... | collective-permute-start | bytes 184328 | tf_op jit(solution)/shard_map/ppermute | solution.py:22
  342.4 15.9 %collective-permute-start.2 = (bf16[1,15,2048]{2,0,1:T(2,128)(2,1)S(1)}, bf16[1,15,2048]{2,0,1:T(2,128)(2,1)S(1)}, u32[]{:S(2)}, u32[]{:S(2)}) collective-permute-start(bf16[1,15,2048]{2,0,1:T(2,128)(2,1)S(1)} %get-tuple-element.20), channel_id=1, source_target_pairs={{0,32},{32,64},{64,96},{96,128},{128,160},{160,192},{192,224},{1,3... | collective-permute-start | bytes 184328 | tf_op jit(solution)/shard_map/ppermute | solution.py:20
  356.2 2.2 copy-start.19
  358.3 5.9 copy-start
  366.5 2.2 copy-start.4
  370.8 347.0 %all-reduce.4.cloned.1.call-start = ((), (), s32[]{:S(2)}) async-start(), calls=%async_computation.5 | async-start | bytes 17301504
  373.6 2.0 copy-start.29
  374.0 2.7 copy-start.5
  374.0 2.7 copy-start.28
  380.7 2.0 copy-start.10
  387.2 44.4 %copy-start.12 = (f32[1024,128]{1,0:T(8,128)S(1)}, f32[1024,128]{1,0:T(8,128)}, u32[]{:S(2)}) copy-start(f32[1024,128]{1,0:T(8,128)} %fusion.8) | copy-start | bytes 1572868
  387.2 44.4 %copy-start.21 = (bf16[1,128,1024]{2,1,0:T(8,128)(2,1)S(1)}, bf16[1,128,1024]{2,1,0:T(8,128)(2,1)}, u32[]{:S(2)}) copy-start(bf16[1,128,1024]{2,1,0:T(8,128)(2,1)} %param.8) | copy-start | bytes 786436
  388.2 45.7 %copy-start.13 = (f32[1024,128]{1,0:T(8,128)S(1)}, f32[1024,128]{1,0:T(8,128)}, u32[]{:S(2)}) copy-start(f32[1024,128]{1,0:T(8,128)} %fusion.12) | copy-start | bytes 1572868
  431.6 4.4 copy-start.1
  450.9 2.0 copy-start.14
  450.9 2.3 copy-start.15
  450.9 2.7 copy-start.16
  451.2 2.7 copy-start.17
  451.5 2.7 copy-start.18
  (8 other events, 11.1 us)
Sparse Core Ops, SparseCore 0:
  10.6 60.5 all-gather.11
  73.8 59.5 all-gather.13
  136.0 58.8 all-gather.15
  198.5 115.0 all-gather.17
  370.9 60.7 all-gather.9
  437.2 280.5 all-reduce.3
where the time goes:
time: 729 us; the launch traced here: 728 us
  waiting for transfers between devices  486 us (67%)
  matrix products  95.1 us (13%)
  blocking collectives  86.5 us (12%)
  local copies, waits for them, and re-layouts  24.2 us (3%)
  starting transfers between devices  14.8 us (2%)
  between operations  14.6 us (2%)
    unnamed x7, waiting for transfers between devices  265 us
    all_gather x1, waiting for transfers between devices, shards(): lax.all_gather(out_weight, ('fsdp', 'frame'), axis=0, tiled=True)  109 us
    all_gather x1, waiting for transfers between devices, shards(): lax.all_gather(own_keys, 'fsdp', axis=0, tiled=True)  53.3 us
    all_gather x1, waiting for transfers between devices, shards(): lax.all_gather(own_queries, 'fsdp', axis=0, tiled=True)  49.5 us
    all_gather x1, blocking collectives, shards(): lax.all_gather(row_dot_table, 'fsdp', axis=0, tiled=True)  30.5 us
    all_gather x1, blocking collectives, shards(): lax.all_gather(row_maxes, 'fsdp', axis=0, tiled=True)  28.1 us
    all_gather x1, blocking collectives, shards(): lax.all_gather(row_totals, 'fsdp', axis=0, tiled=True)  27.9 us
    dot_general x16, matrix products, head_scores(): jnp.einsum('qd,kd->qk', queries, key_rows, preferred_element_type=jnp.flo...  21.8 us
  transfers between devices with their start and end apart: 10, of which 5 were waited for; matrix products, arithmetic and copies ran while one was open for 12% of the time, Pallas kernels for 0%

commit v1 on v0

--- a/solution.py
+++ b/solution.py
@@ -92,7 +92,9 @@
     full_weight = lax.all_gather(out_weight, ("fsdp", "frame"), axis=0, tiled=True)
     groups = lax.axis_size("fsdp")
     all_keys, all_values = (
-        lax.all_gather(own_keys, "fsdp", axis=0, tiled=True),
+        jnp.concatenate(
+            lax.all_to_all(jnp.stack([own_keys] * lax.axis_size("fsdp")), "fsdp", 0, 0), axis=0
+        ),
         lax.all_gather(own_values, "fsdp", axis=0, tiled=True),
     )
     pieces = []

time: 729 us -> 680 us (0.933)
  waiting for transfers between devices: 486 us -> 428 us
    all_gather x1 -> x0, waiting for transfers between devices: 53.3 us -> none  [shards(): lax.all_gather(own_keys, 'fsdp', axis=0, tiled=True)]
    all_gather x1, waiting for transfers between devices: 49.5 us -> 18.9 us  [shards(): lax.all_gather(own_queries, 'fsdp', axis=0, tiled=True)]
    all_to_all x0 -> x1, waiting for transfers between devices: none -> 26.6 us  [shards(): lax.all_to_all(jnp.stack([own_keys] * lax.axis_size('fsdp')), 'fsdp', 0, 0)]
    unnamed x65 -> x179, local copies, waits for them, and re-layouts: 15.9 us -> 17.2 us
    unnamed x7 -> x6, waiting for transfers between devices: 265 us -> 264 us
  transfers between devices with their start and end apart: 10 -> 10, of which waited for: 5 -> 5; matrix products, arithmetic and copies ran while one was open for 12% -> 13% of each run, Pallas kernels for 0% -> 0%
where the time goes in v1:
time: 680 us; the launch traced here: 679 us
  waiting for transfers between devices  428 us (63%)
  matrix products  95 us (14%)
  blocking collectives  86.3 us (13%)
  local copies, waits for them, and re-layouts  26.4 us (4%)
  starting transfers between devices  21.5 us (3%)
  between operations  14.8 us (2%)
    unnamed x6, waiting for transfers between devices  264 us
    all_gather x1, waiting for transfers between devices, shards(): lax.all_gather(out_weight, ('fsdp', 'frame'), axis=0, tiled=True)  109 us
    all_gather x1, blocking collectives, shards(): lax.all_gather(row_dot_table, 'fsdp', axis=0, tiled=True)  30.4 us
    all_gather x1, blocking collectives, shards(): lax.all_gather(row_totals, 'fsdp', axis=0, tiled=True)  27.9 us
    all_gather x1, blocking collectives, shards(): lax.all_gather(row_maxes, 'fsdp', axis=0, tiled=True)  27.9 us
    all_to_all x1, waiting for transfers between devices, shards(): lax.all_to_all(jnp.stack([own_keys] * lax.axis_size('fsdp')), 'fsdp', 0, 0)  26.6 us
    dot_general x16, matrix products, head_scores(): jnp.einsum('qd,kd->qk', queries, key_rows, preferred_element_type=jnp.flo...  22.6 us
    conv_general_dilated x3, matrix products, depthwise(): lax.conv_general_dilated(signal[None], taps[:, None, :], (1,), 'VALID', d...  20.4 us
  transfers between devices with their start and end apart: 10, of which 5 were waited for; matrix products, arithmetic and copies ran while one was open for 13% of the time, Pallas kernels for 0%

profile of v1, /device:TPU:97, one launch (start us, length us, event | category | flops | bytes accessed | tf_op | source)
XLA Modules:
  0.0 678.9 jit_solution(17640064103976226637)
XLA Ops:
  8.6 2.5 stack.8
  11.2 6.8 all-to-all-start
  18.8 5.0 rev.3
  23.8 26.6 %all-to-all-done = bf16[8,128,1024]{2,1,0:T(8,128)(2,1)S(1)} async-done(((bf16[8,128,1024]{2,1,0:T(8,128)(2,1)}), bf16[8,128,1024]{2,1,0:T(8,128)(2,1)S(1)}, u32[]{:S(2)}, u32[]{:S(2)}) %all-to-all-start) | async-done | bytes 2097184 | tf_op jit(solution)/shard_map/all_to_all | solution.py:96
  64.6 27.9 %all_gather.25 = f32[1024,8]{0,1:T(8,128)S(1)} all-gather(f32[128,8]{0,1:T(8,128)S(1)} %stack.10), channel_id=1, replica_groups=mesh['fsdp'=8,'frame'=32] {'fsdp'}, dimensions={0}, use_global_device_ids=true | all-gather | bytes 36864 | tf_op jit(solution)/shard_map/all_gather | solution.py:167
  92.5 27.9 %all_gather.24 = f32[1024,8]{0,1:T(8,128)S(1)} all-gather(f32[128,8]{0,1:T(8,128)S(1)} %stack.9), channel_id=1, replica_groups=mesh['fsdp'=8,'frame'=32] {'fsdp'}, dimensions={0}, use_global_device_ids=true | all-gather | bytes 36864 | tf_op jit(solution)/shard_map/all_gather | solution.py:166
  127.0 18.9 %all-gather.12.cloned.1.call-done = bf16[1,1024,1024]{2,1,0:T(8,128)(2,1)} async-done(((bf16[1,128,1024]{2,1,0:T(8,128)(2,1)}), bf16[1,1024,1024]{2,1,0:T(8,128)(2,1)}) %all-gather.12.cloned.1.call-update) | async-done | bytes 2097168 | tf_op jit(solution)/shard_map/all_gather | solution.py:162
  146.0 2.3 fusion.8
  156.2 108.7 %all-gather.14.cloned.1.call-done = bf16[256,4,2048]{2,1,0:T(4,128)(2,1)} async-done(((bf16[1,4,2048]{2,1,0:T(4,128)(2,1)}), bf16[256,4,2048]{2,1,0:T(4,128)(2,1)}) %all-gather.14.cloned.1.call-update) | async-done | bytes 4194320 | tf_op jit(solution)/shard_map/all_gather | solution.py:92
  264.9 6.9 %reshape.109 = bf16[1024,2048]{1,0:T(8,128)(2,1)} reshape(bf16[256,4,2048]{2,1,0:T(4,128)(2,1)} %all-gather.14.cloned.1.call-done) | data formatting | bytes 8388608
  271.8 2.9 convolution_convert_fusion
  276.2 5.5 collective-permute-start
  281.8 2.2 fusion.36
  284.1 8.1 %multiply_convert_fusion = (bf16[1,128,2048]{2,0,1:T(2,128)(2,1)S(1)}, f32[1,128,2048]{2,0,1:T(1,128)S(1)}) fusion(bf16[1,128,2048]{2,1,0:T(8,128)(2,1)S(1)} %copy-done.83, bf16[31,1,2048]{2,0,1:T(8,128)(2,1)S(1)} %bitcast.164, bf16[1,158,2048]{2,1,0:T(8,128)(2,1)S(1)} %pad_maximum_fusion), kind=kOutput, calls=%fused_computation.178 | convolution fusion | flops 18874368 | bytes 2871296 | tf_op jit(solution)/shard_map/conv_general_dilated | solution.py:72
  293.8 6.3 collective-permute-start.2
  300.2 7.4 %fusion.119 = f32[1,31,2048]{2,0,1:T(1,128)S(1)} fusion(f32[1,128,2048]{2,0,1:T(1,128)S(1)} %get-tuple-element.65, bf16[1,158,2048]{2,1,0:T(8,128)(2,1)S(1)} %pad_maximum_fusion, bf16[1,128,2048]{2,1,0:T(8,128)(2,1)S(1)} %copy-done.83), kind=kOutput, calls=%fused_computation.176 | convolution fusion | flops 18874368 | bytes 2473984 | tf_op jit(solution)/shard_map/conv_general_dilated | solution.py:72
  309.8 4.9 fusion
  315.7 2.3 convolution_convert_fusion.1
  318.0 2.2 multiply_reduce_fusion.7
  320.2 2.0 multiply_reduce_fusion.6
  334.3 4.6 fusion.126
  342.8 30.4 %all_gather.27 = f32[1024,8]{0,1:T(8,128)S(1)} all-gather(f32[128,8]{0,1:T(8,128)S(1)} %stack.11), channel_id=1, replica_groups=mesh['fsdp'=8,'frame'=32] {'fsdp'}, dimensions={0}, use_global_device_ids=true | all-gather | bytes 36864 | tf_op jit(solution)/shard_map/all_gather | solution.py:168
  373.3 9.8 %all-gather.8.cloned.1.call-done = bf16[1024,1024]{1,0:T(8,128)(2,1)} async-done(((bf16[128,1024]{1,0:T(8,128)(2,1)}), bf16[1024,1024]{1,0:T(8,128)(2,1)}) %all-gather.8.cloned.1.call-update) | async-done | bytes 2097168 | tf_op jit(solution)/shard_map/all_gather | solution.py:163
  383.1 2.4 fusion.63
  385.5 2.3 fusion.65
  387.8 2.0 fusion.67
  389.8 2.2 fusion.69
  392.0 2.0 fusion.71
  394.0 2.3 fusion.73
  396.3 2.2 fusion.75
  398.5 2.2 fusion.77
  406.9 262.3 %all-reduce.4.cloned.1.call-done = (f32[1024,2048]{1,0:T(8,128)}, f32[31,2048]{1,0:T(8,128)}) async-done(((f32[1024,2048]{1,0:T(8,128)}, f32[31,2048]{1,0:T(8,128)}), (f32[1024,2048]{1,0:T(8,128)}, f32[31,2048]{1,0:T(8,128)})) %all-reduce.4.cloned.1.call-update) | async-done | bytes 8642576
  (259 shorter events, 61.9 us)
Async XLA Ops:
  7.2 114.6 %all-gather.10.cloned.1.call-start = ((), (), s32[]{:S(2)}) async-start(), calls=%async_computation.2 | async-start | bytes 2359296 | tf_op jit(solution)/shard_map/all_gather | solution.py:98
  7.9 138.1 %all-gather.12.cloned.1.call-start = ((), (), s32[]{:S(2)}) async-start(), calls=%async_computation.3 | async-start | bytes 2359296 | tf_op jit(solution)/shard_map/all_gather | solution.py:162
  11.2 7.6 %copy-start.33 = (bf16[31,2048]{1,0:T(8,128)(2,1)S(1)}, bf16[31,2048]{1,0:T(8,128)(2,1)}, u32[]{:S(2)}) copy-start(bf16[31,2048]{1,0:T(8,128)(2,1)} %param.10) | copy-start | bytes 380932
  11.2 39.2 %all-to-all-start = ((bf16[8,128,1024]{2,1,0:T(8,128)(2,1)}), bf16[8,128,1024]{2,1,0:T(8,128)(2,1)S(1)}, u32[]{:S(2)}, u32[]{:S(2)}) async-start(bf16[8,128,1024]{2,1,0:T(8,128)(2,1)} %stack.8), calls=%async_computation | async-start | bytes 4194304 | tf_op jit(solution)/shard_map/all_to_all | solution.py:96
  18.0 246.9 %all-gather.14.cloned.1.call-start = ((), (), s32[]{:S(2)}) async-start(), calls=%async_computation.4 | async-start | bytes 4210688 | tf_op jit(solution)/shard_map/all_gather | solution.py:92
  18.7 364.4 %all-gather.8.cloned.1.call-start = ((), (), s32[]{:S(2)}) async-start(), calls=%async_computation.1 | async-start | bytes 2359296 | tf_op jit(solution)/shard_map/all_gather | solution.py:163
  53.0 11.6 %copy-start.43 = (f32[128]{0:T(128)}, f32[128]{0:T(128)S(1)}, u32[]{:S(2)}) copy-start(f32[128]{0:T(128)S(1)} %get-tuple-element.48) | copy-start | bytes 1540
  53.2 10.8 %copy-start.78 = (f32[128]{0:T(128)}, f32[128]{0:T(128)S(1)}, u32[]{:S(2)}) copy-start(f32[128]{0:T(128)S(1)} %fusion.132) | copy-start | bytes 1540
  54.5 10.1 %copy-start.40 = (f32[128]{0:T(128)}, f32[128]{0:T(128)S(1)}, u32[]{:S(2)}) copy-start(f32[128]{0:T(128)S(1)} %get-tuple-element.50) | copy-start | bytes 1540
  54.7 9.3 %copy-start.75 = (f32[128]{0:T(128)}, f32[128]{0:T(128)S(1)}, u32[]{:S(2)}) copy-start(f32[128]{0:T(128)S(1)} %fusion.134) | copy-start | bytes 1540
  56.0 8.5 %copy-start.37 = (f32[128]{0:T(128)}, f32[128]{0:T(128)S(1)}, u32[]{:S(2)}) copy-start(f32[128]{0:T(128)S(1)} %get-tuple-element.52) | copy-start | bytes 1540
  56.0 266.3 %copy-start.10 = (f32[128,1024]{1,0:T(8,128)}, f32[128,1024]{1,0:T(8,128)S(1)}, u32[]{:S(2)}) copy-start(f32[128,1024]{1,0:T(8,128)S(1)} %get-tuple-element.53) | copy-start | bytes 1572868
  56.3 7.8 %copy-start.72 = (f32[128]{0:T(128)}, f32[128]{0:T(128)S(1)}, u32[]{:S(2)}) copy-start(f32[128]{0:T(128)S(1)} %fusion.136) | copy-start | bytes 1540
  57.6 266.2 %copy-start.8 = (f32[128,1024]{1,0:T(8,128)}, f32[128,1024]{1,0:T(8,128)S(1)}, u32[]{:S(2)}) copy-start(f32[128,1024]{1,0:T(8,128)S(1)} %get-tuple-element.55) | copy-start | bytes 1572868
  59.1 265.4 %copy-start.6 = (f32[128,1024]{1,0:T(8,128)}, f32[128,1024]{1,0:T(8,128)S(1)}, u32[]{:S(2)}) copy-start(f32[128,1024]{1,0:T(8,128)S(1)} %get-tuple-element.57) | copy-start | bytes 1572868
  59.4 61.7 %copy-start.66 = (f32[128]{0:T(128)}, f32[128]{0:T(128)S(1)}, u32[]{:S(2)}) copy-start(f32[128]{0:T(128)S(1)} %fusion.140) | copy-start | bytes 1540
  60.7 264.2 %copy-start.4 = (f32[128,1024]{1,0:T(8,128)}, f32[128,1024]{1,0:T(8,128)S(1)}, u32[]{:S(2)}) copy-start(f32[128,1024]{1,0:T(8,128)S(1)} %get-tuple-element.59) | copy-start | bytes 1572868
  60.9 60.8 %copy-start.63 = (f32[128]{0:T(128)}, f32[128]{0:T(128)S(1)}, u32[]{:S(2)}) copy-start(f32[128]{0:T(128)S(1)} %fusion.142) | copy-start | bytes 1540
  62.4 59.3 %copy-start.60 = (f32[128]{0:T(128)}, f32[128]{0:T(128)S(1)}, u32[]{:S(2)}) copy-start(f32[128]{0:T(128)S(1)} %fusion.144) | copy-start | bytes 1540
  271.8 9.9 %copy-start.45 = (f32[1024,1]{0,1:T(1,128)S(1)}, f32[1024,1]{0,1:T(1,128)}, u32[]{:S(2)}) copy-start(f32[1024,1]{0,1:T(1,128)} %get-tuple-element.40) | copy-start | bytes 12292
  271.8 9.9 %copy-start.46 = (f32[1024,1]{0,1:T(1,128)S(1)}, f32[1024,1]{0,1:T(1,128)}, u32[]{:S(2)}) copy-start(f32[1024,1]{0,1:T(1,128)} %get-tuple-element.32) | copy-start | bytes 12292
  274.8 9.4 %copy-start.83 = (bf16[1,128,2048]{2,1,0:T(8,128)(2,1)S(1)}, bf16[1,128,2048]{2,1,0:T(8,128)(2,1)}, u32[]{:S(2)}) copy-start(bf16[1,128,2048]{2,1,0:T(8,128)(2,1)} %param.11) | copy-start | bytes 1572868
  274.8 9.1 %collective-permute-start.1 = (bf16[1,15,2048]{2,1,0:T(8,128)(2,1)S(1)}, bf16[1,15,2048]{2,1,0:T(8,128)(2,1)S(1)}, u32[]{:S(2)}, u32[]{:S(2)}) collective-permute-start(bf16[1,15,2048]{2,1,0:T(8,128)(2,1)S(1)} %get-tuple-element.23), channel_id=1, source_target_pairs={{32,0},{64,32},{96,64},{128,96},{160,128},{192,160},{224,192},{33,... | collective-permute-start | bytes 184328 | tf_op jit(solution)/shard_map/ppermute | solution.py:22
  276.2 7.7 %collective-permute-start = (bf16[1,15,2048]{2,1,0:T(8,128)(2,1)S(1)}, bf16[1,15,2048]{2,1,0:T(8,128)(2,1)S(1)}, u32[]{:S(2)}, u32[]{:S(2)}) collective-permute-start(bf16[1,15,2048]{2,1,0:T(8,128)(2,1)S(1)} %get-tuple-element.22), channel_id=1, source_target_pairs={{0,32},{32,64},{64,96},{96,128},{128,160},{160,192},{192,224},{1,3... | collective-permute-start | bytes 184328 | tf_op jit(solution)/shard_map/ppermute | solution.py:20
  292.5 17.2 %collective-permute-start.3 = (bf16[1,15,2048]{2,0,1:T(2,128)(2,1)S(1)}, bf16[1,15,2048]{2,0,1:T(2,128)(2,1)S(1)}, u32[]{:S(2)}, u32[]{:S(2)}) collective-permute-start(bf16[1,15,2048]{2,0,1:T(2,128)(2,1)S(1)} %get-tuple-element.21), channel_id=1, source_target_pairs={{32,0},{64,32},{96,64},{128,96},{160,128},{192,160},{224,192},{33,... | collective-permute-start | bytes 184328 | tf_op jit(solution)/shard_map/ppermute | solution.py:22
  293.8 15.9 %collective-permute-start.2 = (bf16[1,15,2048]{2,0,1:T(2,128)(2,1)S(1)}, bf16[1,15,2048]{2,0,1:T(2,128)(2,1)S(1)}, u32[]{:S(2)}, u32[]{:S(2)}) collective-permute-start(bf16[1,15,2048]{2,0,1:T(2,128)(2,1)S(1)} %get-tuple-element.20), channel_id=1, source_target_pairs={{0,32},{32,64},{64,96},{96,128},{128,160},{160,192},{192,224},{1,3... | collective-permute-start | bytes 184328 | tf_op jit(solution)/shard_map/ppermute | solution.py:20
  322.3 346.9 %all-reduce.4.cloned.1.call-start = ((), (), s32[]{:S(2)}) async-start(), calls=%async_computation.5 | async-start | bytes 17301504
  338.9 44.2 %copy-start.32 = (bf16[1,128,1024]{2,1,0:T(8,128)(2,1)S(1)}, bf16[1,128,1024]{2,1,0:T(8,128)(2,1)}, u32[]{:S(2)}) copy-start(bf16[1,128,1024]{2,1,0:T(8,128)(2,1)} %param.8) | copy-start | bytes 786436
  340.9 46.9 %copy-start.23 = (f32[1024,128]{1,0:T(8,128)S(1)}, f32[1024,128]{1,0:T(8,128)}, u32[]{:S(2)}) copy-start(f32[1024,128]{1,0:T(8,128)} %fusion.16) | copy-start | bytes 1572868
  383.1 8.9 %copy-start.25 = (f32[1024,128]{1,0:T(8,128)S(1)}, f32[1024,128]{1,0:T(8,128)}, u32[]{:S(2)}) copy-start(f32[1024,128]{1,0:T(8,128)} %fusion.24) | copy-start | bytes 1572868
  394.0 8.4 %copy-start.21 = (f32[1024,128]{1,0:T(8,128)S(1)}, f32[1024,128]{1,0:T(8,128)}, u32[]{:S(2)}) copy-start(f32[1024,128]{1,0:T(8,128)} %fusion.8) | copy-start | bytes 1572868
  394.0 8.7 %copy-start.22 = (f32[1024,128]{1,0:T(8,128)S(1)}, f32[1024,128]{1,0:T(8,128)}, u32[]{:S(2)}) copy-start(f32[1024,128]{1,0:T(8,128)} %fusion.12) | copy-start | bytes 1572868
  (65 other events, 161.5 us)
Sparse Core Ops, SparseCore 0:
  10.6 73.7 all-gather.9
  87.1 58.8 all-gather.11
  149.7 115.1 all-gather.13
  322.4 60.6 all-gather.7
  388.6 280.5 all-reduce.3
